TPU v7x, 256 devices: a whole 4x4x8 slice. The times are simulated.
256 devices in a mesh: frame: 16 (over y, z_hi, core), row: 16 (over x, z_lo).
Axes of the slice: x: 4, y: 4, z: 8 (z_hi: 2, z_lo: 4; z = z_hi * 4 + z_lo), core: 2. Of those that a mesh axis runs over, the one named last changes fastest.
Arguments:
- spatial_q: bfloat16 [32, 128, 32, 1152], P('frame', 'row'), may hold values from -10.5 to 10.5
- spatial_k: bfloat16 [32, 128, 32, 1152], P('frame', 'row'), may hold values from -10.5 to 10.5
- spatial_v: bfloat16 [32, 128, 32, 1152], P('frame', 'row'), may hold values from -6 to 6
- residual: bfloat16 [32, 128, 32, 1152], P('frame', 'row'), may hold values from -6 to 6
- neighbour_list: int32 [64, 6], P('row'), may hold values from 0 to 15, as said below
- block_mask: int32 [8, 8], replicated, may hold values from 0 to 1, as said below
- out_weight: bfloat16 [1152, 1152], P('frame'), may hold values from -0.1875 to 0.1875
- qkv_weight: bfloat16 [1152, 3456], P('frame'), may hold values from -1.4799 to 1.4799
- pos_embed: float32 [32, 1152], P('frame'), may hold values from -150.5 to 150.5
- mod_shift: float32 [1152], replicated, may hold values from -2 to 2
- mod_scale: float32 [1152], replicated, may hold values from -2 to 2
Outputs:
- temporal_mix: bfloat16 [32, 128, 32, 1152], P('frame', 'row')
Inputs may be any that keep to these rules, and one draw needn't show every extreme that they name: `neighbour_list`: each row holds 6 different tiles of its own clip: slot 0 is the row's own tile; every other lies at most one tile row and at most two tile columns away from it, inside the grid of 16 tiles. `block_mask`: entry (i, j) is 1 where i == j and 0 where j > i.
All inputs are finite; a program needn't handle non-finite values.
Results may differ from a plain program's by a relative error of at most 0.0056.
The roundings to bfloat16 on the way count: a program that leaves them out, or rounds other values in their place, can miss the bound.
Values may be sent and summed in bfloat16 or wider, within the bound.
No kernel may reach another device: no remote copies, remote signals or barrier semaphores. Data moves between devices by JAX's collectives and lax.ppermute only.
A program may use at most 128 MiB of HBM per device.

v0:
```python
import math

import jax
import jax.numpy as jnp
from jax import lax
from jax.sharding import PartitionSpec as P

HEADS = 16
TILE = 8
SLOTS = 6
ROWS = 32
BLOCK = 4


EPS = 1e-06


def padded(block, sides, width):
    for axis, dim in sides:
        count = lax.axis_size(axis)
        forward = [(i, i + 1) for i in range(count - 1)]
        forward.append((count - 1, 0))
        backward = [(target, source) for source, target in forward]
        low = lax.ppermute(
            lax.slice_in_dim(block, block.shape[dim] - width, None, axis=dim), axis, forward
        )
        high = lax.ppermute(lax.slice_in_dim(block, 0, width, axis=dim), axis, backward)
        block = jnp.concatenate([low, block, high], axis=dim)
    return block


def tiles_of(field):
    leading = field.shape[:-3]
    height, breadth, channels = field.shape[-3:]
    tile_grid = field.reshape(leading + (height // TILE, TILE, breadth // TILE, TILE, channels))
    lead_count = len(leading)
    arrangement = tuple(range(lead_count)) + (
        lead_count,
        lead_count + 2,
        lead_count + 1,
        lead_count + 3,
        lead_count + 4,
    )
    tile_grid = jnp.transpose(tile_grid, arrangement)
    return tile_grid.reshape(leading + (height // TILE * (breadth // TILE), TILE * TILE, channels))


def untile(tiles, height, breadth):
    leading = tiles.shape[:-3]
    channels = tiles.shape[-1]
    tile_grid = tiles.reshape(leading + (height // TILE, breadth // TILE, TILE, TILE, channels))
    lead_count = len(leading)
    arrangement = tuple(range(lead_count)) + (
        lead_count,
        lead_count + 2,
        lead_count + 1,
        lead_count + 3,
        lead_count + 4,
    )
    return jnp.transpose(tile_grid, arrangement).reshape(leading + (height, breadth, channels))


def window_attention(queries, keys, values):
    tile_count, token_count, channels = queries.shape
    head_size = channels // HEADS
    shaped_q = queries.reshape(tile_count, token_count, HEADS, head_size)
    shaped_k = keys.reshape(tile_count, -1, HEADS, head_size)
    shaped_v = values.reshape(tile_count, -1, HEADS, head_size)
    scores = jnp.einsum(
        "tqhe,tkhe->thqk", shaped_q, shaped_k, preferred_element_type=jnp.float32
    ) * (1.0 / math.sqrt(head_size))
    peak = jnp.max(scores, axis=-1, keepdims=True)
    powers = jnp.exp(scores - peak)
    weights = (powers / jnp.sum(powers, axis=-1, keepdims=True)).astype(jnp.bfloat16)
    mixed = jnp.einsum("thqk,tkhe->tqhe", weights, shaped_v, preferred_element_type=jnp.float32)
    return mixed.astype(jnp.bfloat16).reshape(tile_count, token_count, channels)


def frame_attention(queries, keys, values, allowed):
    frame_count, spot_count, channels = queries.shape
    head_size = channels // HEADS
    shaped_q = queries.reshape(frame_count, spot_count, HEADS, head_size)
    shaped_k = keys.reshape(frame_count, spot_count, HEADS, head_size)
    shaped_v = values.reshape(frame_count, spot_count, HEADS, head_size)
    scores = jnp.einsum(
        "fphe,gphe->phfg", shaped_q, shaped_k, preferred_element_type=jnp.float32
    ) * (1.0 / math.sqrt(head_size))
    scores = jnp.where(allowed, scores, -jnp.inf)
    peak = jnp.max(scores, axis=-1, keepdims=True)
    powers = jnp.exp(scores - peak)
    weights = (powers / jnp.sum(powers, axis=-1, keepdims=True)).astype(jnp.bfloat16)
    mixed = jnp.einsum("phfg,gphe->fphe", weights, shaped_v, preferred_element_type=jnp.float32)
    return mixed.astype(jnp.bfloat16).reshape(frame_count, spot_count, channels)


def normalize(field, mod_shift, mod_scale):
    average = jnp.mean(field, axis=-1, keepdims=True)
    centred = field - average
    spread = jnp.mean(centred * centred, axis=-1, keepdims=True)
    return centred * lax.rsqrt(spread + EPS) * (1.0 + mod_scale) + mod_shift


def fold_with(left, piece):
    return jnp.dot(left, piece, preferred_element_type=jnp.float32)


def frame_window(items):
    return window_attention(items[0], items[1], items[2])


def local(
    spatial_q,
    spatial_k,
    spatial_v,
    residual,
    neighbour_list,
    block_mask,
    out_weight,
    qkv_weight,
    pos_embed,
    mod_shift,
    mod_scale,
):
    frames_here, height, breadth, channels = spatial_q.shape
    tiles_wide = breadth // TILE
    tokens_here = frames_here * height * breadth
    stacked = jnp.stack((spatial_k, spatial_v), 0)
    rims = padded(stacked, (("row", 2),), TILE)
    key_tiles = tiles_of(rims)
    tile_row_here = (lax.axis_index("row") + 1) % (ROWS // TILE)
    local_ids = (
        (neighbour_list // tiles_wide - tile_row_here + 1) * tiles_wide
        + neighbour_list % tiles_wide
    ).reshape(-1)
    picked = jnp.take(key_tiles, local_ids, axis=2).reshape(
        2, frames_here, tiles_wide, SLOTS * TILE * TILE, channels
    )
    query_tiles = tiles_of(spatial_q)
    attended = lax.map(frame_window, (query_tiles, picked[0], picked[1]))
    heads = untile(attended, height, breadth).reshape(tokens_here, channels)
    spatial_sum = fold_with(heads, lax.all_gather(out_weight, "frame", axis=0, tiled=True))
    mixed = (residual.reshape(tokens_here, channels).astype(jnp.float32) + spatial_sum).astype(
        jnp.bfloat16
    )
    mixed = lax.optimization_barrier(mixed)
    shifted = (
        mixed.astype(jnp.float32).reshape(frames_here, height * breadth, channels)
        + pos_embed[:, None, :]
    )
    normed = normalize(shifted, mod_shift, mod_scale).astype(jnp.bfloat16)
    normed_rows = normed.reshape(tokens_here, channels)
    projected = fold_with(
        normed_rows, lax.all_gather(qkv_weight, "frame", axis=0, tiled=True)
    ).astype(jnp.bfloat16)
    projected = projected.reshape(frames_here, height * breadth, 3 * channels)
    projected = lax.all_to_all(projected, "frame", split_axis=1, concat_axis=0, tiled=True)
    allowed = jnp.repeat(jnp.repeat(block_mask, BLOCK, axis=0), BLOCK, axis=1) == 1
    temporal = frame_attention(
        projected[..., :channels],
        projected[..., channels : 2 * channels],
        projected[..., 2 * channels :],
        allowed,
    )
    returned = lax.all_to_all(temporal, "frame", split_axis=0, concat_axis=1, tiled=True)
    return returned.reshape(frames_here, height, breadth, channels)


def solution(mesh):
    return jax.shard_map(
        local,
        mesh=mesh,
        in_specs=(
            P("frame", "row", None, None),
            P("frame", "row", None, None),
            P("frame", "row", None, None),
            P("frame", "row", None, None),
            P("row", None),
            P(),
            P("frame", None),
            P("frame", None),
            P("frame", None),
            P(),
            P(),
        ),
        out_specs=P("frame", "row", None, None),
        check_vma=False,
    )
```

profile of v0, /device:TPU:38, one launch (start us, length us, event | category | flops | bytes accessed | tf_op | source)
XLA Modules:
  0.0 433.2 jit_solution(16643806574621268661)
XLA Ops:
  17.2 108.4 %collective-permute-done = bf16[2,2,8,32,1152]{4,3,2,1,0:T(8,128)(2,1)} collective-permute-done((bf16[2,2,8,32,1152]{4,3,2,1,0:T(8,128)(2,1)}, bf16[2,2,8,32,1152]{4,3,2,1,0:T(8,128)(2,1)}, u32[]{:S(2)}, u32[]{:S(2)}) %collective-permute-start) | collective-permute-done | bytes 2359328 | tf_op jit(solution)/shard_map/ppermute | solution.py:24
  125.6 9.0 %collective-permute-done.1 = bf16[2,2,8,32,1152]{4,3,2,1,0:T(8,128)(2,1)} collective-permute-done((bf16[2,2,8,32,1152]{4,3,2,1,0:T(8,128)(2,1)}, bf16[2,2,8,32,1152]{4,3,2,1,0:T(8,128)(2,1)}, u32[]{:S(2)}, u32[]{:S(2)}) %collective-permute-start.1) | collective-permute-done | bytes 2359328 | tf_op jit(solution)/shard_map/ppermute | solution.py:27
  134.7 3.5 pad_maximum_fusion
  138.1 4.0 copy.47
  142.1 9.7 %gather_fusion = bf16[24,2,2,64,1152]{4,3,2,1,0:T(8,128)(2,1)} fusion(bf16[2,2,12,64,1152]{4,3,2,1,0:T(8,128)(2,1)} %bitcast.78, s32[1024]{0:T(1024)S(1)} %pad_clamp_fusion), kind=kCustom, calls=%fused_computation | custom fusion | bytes 28311648 | tf_op jit(solution)/shard_map/jit(_take)/gather | solution.py:135
  151.8 7.0 %select_bitcast_fusion = bf16[2,2,24,64,1152]{4,3,1,0,2:T(8,128)(2,1)S(1)} fusion(bf16[24,2,2,64,1152]{4,3,2,1,0:T(8,128)(2,1)} %gather_fusion, pred[24]{0:T(512)(128)(4,1)S(1)} %copy-done.13), kind=kLoop, calls=%fused_computation.18 | loop fusion | flops 7077888 | bytes 28311576 | tf_op jit(solution)/shard_map/jit(_take)/select_n | solution.py:135
  160.4 3.6 copy.48
  164.0 3.6 copy.50
  167.6 74.2 %while.10 = (s32[]{:T(128)}, bf16[2,4,64,1152]{3,2,1,0:T(8,128)(2,1)}, bf16[2,4,384,1152]{3,2,1,0:T(8,128)(2,1)}, bf16[2,4,64,1152]{3,2,1,0:T(8,128)(2,1)}, bf16[2,4,384,1152]{3,2,1,0:T(8,128)(2,1)}, /*index=5*/s32[]{:T(128)}) while((s32[]{:T(128)}, bf16[2,4,64,1152]{3,2,1,0:T(8,128)(2,1)}, bf16[2,4,384,1152]{3,2,1,0:T(8,128)(2,1)}, ...), condition=%wide.region_3.4_spmd, body=%wide.region_0.3_spmd.sunk | while | flops 462717312 | bytes 77103232 | solution.py:139
  168.0 5.5 %constant_dynamic-slice_fusion.5 = (bf16[1,4,384,1152]{3,2,1,0:T(8,128)(2,1)}, bf16[1,4,384,1152]{3,2,1,0:T(8,128)(2,1)S(1)}) fusion(bf16[2,4,384,1152]{3,2,1,0:T(8,128)(2,1)} %get-tuple-element.124, s32[]{:T(128)} %get-tuple-element.114, bf16[2,4,384,1152]{3,2,1,0:T(8,128)(2,1)} %get-tuple-element.122), kind=kLoop, calls=%fused_computation.13.clone.1 | loop fusion | bytes 14155780 | tf_op jit(solution)/shard_map/while/body/jit(dynamic_index_in_dim)/dynamic_slice | solution.py:139
  173.5 5.8 %copy.84 = bf16[1,4,384,1152]{2,3,1,0:T(8,128)(2,1)} copy(bf16[1,4,384,1152]{3,2,1,0:T(8,128)(2,1)} %get-tuple-element.105) | data formatting | bytes 7077888 | tf_op jit(solution)/shard_map/while/body/jit(dynamic_index_in_dim)/dynamic_slice | solution.py:139
  181.2 3.7 reshape.160
  188.2 4.6 %fusion.57 = (f32[4,16,64]{2,1,0:T(8,128)}, f32[4,16,64,384]{3,2,1,0:T(8,128)}) fusion(f32[4,16,64,384]{3,2,1,0:T(8,128)S(1)} %fusion.56), kind=kOutput, calls=%fused_computation.67.clone.1 | output fusion | flops 6291839 | bytes 12599296 | tf_op jit(solution)/shard_map/while/body/eval_jaxpr/sub | solution.py:73
  192.8 3.6 copy.83
  196.5 5.3 %fusion.58 = bf16[4,64,16,72]{3,1,2,0:T(8,128)(2,1)S(1)} fusion(bf16[4,384,16,72]{1,3,2,0:T(8,128)(2,1)} %bitcast.75, f32[4,16,64,384]{3,2,1,0:T(8,128)} %get-tuple-element.106, f32[4,16,64]{2,1,0:T(8,128)} %get-tuple-element.107), kind=kOutput, calls=%fused_computation.9.clone.1 | convolution fusion | flops 229933056 | bytes 10436608 | tf_op jit(solution)/shard_map/while/body/eval_jaxpr/thqk,tkhe->tqhe/dot_general | solution.py:75
  204.8 5.4 %constant_dynamic-slice_fusion.5 = (bf16[1,4,384,1152]{3,2,1,0:T(8,128)(2,1)}, bf16[1,4,384,1152]{3,2,1,0:T(8,128)(2,1)S(1)}) fusion(bf16[2,4,384,1152]{3,2,1,0:T(8,128)(2,1)} %get-tuple-element.124, s32[]{:T(128)} %get-tuple-element.114, bf16[2,4,384,1152]{3,2,1,0:T(8,128)(2,1)} %get-tuple-element.122), kind=kLoop, calls=%fused_computation.13.clone.1 | loop fusion | bytes 14155780 | tf_op jit(solution)/shard_map/while/body/jit(dynamic_index_in_dim)/dynamic_slice | solution.py:139
  210.3 5.8 %copy.84 = bf16[1,4,384,1152]{2,3,1,0:T(8,128)(2,1)} copy(bf16[1,4,384,1152]{3,2,1,0:T(8,128)(2,1)} %get-tuple-element.105) | data formatting | bytes 7077888 | tf_op jit(solution)/shard_map/while/body/jit(dynamic_index_in_dim)/dynamic_slice | solution.py:139
  218.0 3.7 reshape.160
  225.0 4.6 %fusion.57 = (f32[4,16,64]{2,1,0:T(8,128)}, f32[4,16,64,384]{3,2,1,0:T(8,128)}) fusion(f32[4,16,64,384]{3,2,1,0:T(8,128)S(1)} %fusion.56), kind=kOutput, calls=%fused_computation.67.clone.1 | output fusion | flops 6291839 | bytes 12599296 | tf_op jit(solution)/shard_map/while/body/eval_jaxpr/sub | solution.py:73
  229.6 3.6 copy.83
  233.2 5.3 %fusion.58 = bf16[4,64,16,72]{3,1,2,0:T(8,128)(2,1)S(1)} fusion(bf16[4,384,16,72]{1,3,2,0:T(8,128)(2,1)} %bitcast.75, f32[4,16,64,384]{3,2,1,0:T(8,128)} %get-tuple-element.106, f32[4,16,64]{2,1,0:T(8,128)} %get-tuple-element.107), kind=kOutput, calls=%fused_computation.9.clone.1 | convolution fusion | flops 229933056 | bytes 10436608 | tf_op jit(solution)/shard_map/while/body/eval_jaxpr/thqk,tkhe->tqhe/dot_general | solution.py:75
  243.3 3.9 fusion.13
  248.6 4.1 all-gather.5.cloned.1.call-done
  252.7 8.3 %convolution_convert_fusion = bf16[512,3456]{1,0:T(8,128)(2,1)S(1)} fusion(bf16[512,1152]{1,0:T(8,128)(2,1)S(1)} %add_convert_fusion, bf16[1152,3456]{1,0:T(8,128)(2,1)} %all-gather.5.cloned.1.call-done), kind=kOutput, calls=%fused_computation.20 | convolution fusion | flops 4078632960 | bytes 12681216 | tf_op jit(solution)/shard_map/dot_general | solution.py:104
  261.0 5.4 %copy.54 = bf16[2,256,3456]{2,0,1:T(2,128)(2,1)} copy(bf16[2,256,3456]{2,1,0:T(8,128)(2,1)S(1)} %bitcast.87) | data formatting | bytes 7077888 | tf_op jit(solution)/shard_map/reshape | solution.py:155
  266.4 6.1 %all-to-all-start = ((bf16[2,256,3456]{2,0,1:T(2,128)(2,1)}), bf16[2,256,3456]{2,0,1:T(2,128)(2,1)S(1)}, u32[]{:S(2)}, u32[]{:S(2)}) async-start(bf16[2,256,3456]{2,0,1:T(2,128)(2,1)} %copy.54), calls=%async_computation | async-start | bytes 7077888 | tf_op jit(solution)/shard_map/all_to_all | solution.py:156
  272.6 84.6 %all-to-all-done = bf16[2,256,3456]{2,0,1:T(2,128)(2,1)S(1)} async-done(((bf16[2,256,3456]{2,0,1:T(2,128)(2,1)}), bf16[2,256,3456]{2,0,1:T(2,128)(2,1)S(1)}, u32[]{:S(2)}, u32[]{:S(2)}) %all-to-all-start) | async-done | bytes 3538976 | tf_op jit(solution)/shard_map/all_to_all | solution.py:156
  359.5 5.0 %reshape.146 = bf16[32,16,16,72]{3,2,1,0:T(8,128)(2,1)S(1)} reshape(bf16[32,16,1152]{2,1,0:T(8,128)(2,1)} %get-tuple-element.66) | data formatting | bytes 2359296 | tf_op jit(solution)/shard_map/reshape | solution.py:82
  364.5 5.7 %reshape.147 = bf16[32,16,16,72]{3,2,1,0:T(8,128)(2,1)} reshape(bf16[32,16,1152]{2,1,0:T(8,128)(2,1)} %get-tuple-element.65) | data formatting | bytes 2359296 | tf_op jit(solution)/shard_map/reshape | solution.py:83
  370.2 4.7 %reshape.145 = bf16[32,16,16,72]{3,2,1,0:T(8,128)(2,1)} reshape(bf16[32,16,1152]{2,1,0:T(8,128)(2,1)S(1)} %get-tuple-element.64) | data formatting | bytes 2359296 | tf_op jit(solution)/shard_map/reshape | solution.py:84
  374.9 4.3 fusion.18
  386.9 38.1 %all_to_all.33 = bf16[32,16,1152]{2,1,0:T(8,128)(2,1)S(1)} all-to-all(bf16[32,16,1152]{2,1,0:T(8,128)(2,1)} %reshape.148), channel_id=1, replica_groups=mesh['frame'=16,'row'=16] {'frame'}, dimensions={0} | all-to-all | bytes 2359296 | tf_op jit(solution)/shard_map/all_to_all | solution.py:164
  (78 shorter events, 42.7 us)
Async XLA Ops:
  6.5 9.5 %copy-start = (bf16[2,8,32,1152]{3,2,1,0:T(8,128)(2,1)S(1)}, bf16[2,8,32,1152]{3,2,1,0:T(8,128)(2,1)}, u32[]{:S(2)}) copy-start(bf16[2,8,32,1152]{3,2,1,0:T(8,128)(2,1)} %param.13) | copy-start | bytes 3538948
  6.5 236.7 %all-gather.3.cloned.1.call-start = ((), (), s32[]{:S(2)}) async-start(), calls=%async_computation.2 | async-start | bytes 2820096 | tf_op jit(solution)/shard_map/all_gather | solution.py:141
  7.3 6.3 %copy-start.12 = (s32[4,6]{1,0:T(4,128)S(1)}, s32[4,6]{1,0:T(4,128)}, u32[]{:S(2)}) copy-start(s32[4,6]{1,0:T(4,128)} %param.17) | copy-start | bytes 292
  7.3 8.2 %copy-start.10 = (f32[1152]{0:T(1024)S(1)}, f32[1152]{0:T(1024)}, u32[]{:S(2)}) copy-start(f32[1152]{0:T(1024)} %param.23) | copy-start | bytes 13828
  7.3 245.4 %all-gather.5.cloned.1.call-start = ((), (), s32[]{:S(2)}) async-start(), calls=%async_computation.3 | async-start | bytes 8460288 | tf_op jit(solution)/shard_map/all_gather | solution.py:153
  8.0 126.6 %copy-start.2 = (bf16[2,8,32,1152]{3,2,1,0:T(8,128)(2,1)S(1)}, bf16[2,8,32,1152]{3,2,1,0:T(8,128)(2,1)}, u32[]{:S(2)}) copy-start(bf16[2,8,32,1152]{3,2,1,0:T(8,128)(2,1)} %param.15) | copy-start | bytes 3538948
  8.0 126.6 %copy-start.3 = (bf16[2,8,32,1152]{3,2,1,0:T(8,128)(2,1)S(1)}, bf16[2,8,32,1152]{3,2,1,0:T(8,128)(2,1)}, u32[]{:S(2)}) copy-start(bf16[2,8,32,1152]{3,2,1,0:T(8,128)(2,1)} %param.14) | copy-start | bytes 3538948
  11.5 114.1 %collective-permute-start = (bf16[2,2,8,32,1152]{4,3,2,1,0:T(8,128)(2,1)}, bf16[2,2,8,32,1152]{4,3,2,1,0:T(8,128)(2,1)}, u32[]{:S(2)}, u32[]{:S(2)}) collective-permute-start(bf16[2,2,8,32,1152]{4,3,2,1,0:T(8,128)(2,1)} %pad_maximum_fusion.1), channel_id=1, source_target_pairs={{0,1},{1,2},{2,3},{3,4},{4,5},{5,6},{6,7},{7,8},{8,9},{9,10},{10,1... | collective-permute-start | bytes 7077896 | tf_op jit(solution)/shard_map/ppermute | solution.py:24
  13.4 121.2 %collective-permute-start.1 = (bf16[2,2,8,32,1152]{4,3,2,1,0:T(8,128)(2,1)}, bf16[2,2,8,32,1152]{4,3,2,1,0:T(8,128)(2,1)}, u32[]{:S(2)}, u32[]{:S(2)}) collective-permute-start(bf16[2,2,8,32,1152]{4,3,2,1,0:T(8,128)(2,1)} %pad_maximum_fusion.1), channel_id=1, source_target_pairs={{1,0},{2,1},{3,2},{4,3},{5,4},{6,5},{7,6},{8,7},{9,8},{10,9},{11,1... | collective-permute-start | bytes 7077896 | tf_op jit(solution)/shard_map/ppermute | solution.py:27
  142.1 9.7 %copy-start.13 = (pred[24]{0:T(512)(128)(4,1)S(1)}, pred[24]{0:T(512)(128)(4,1)}, u32[]{:S(2)}) copy-start(pred[24]{0:T(512)(128)(4,1)} %compare_and_fusion) | copy-start | bytes 76
  201.7 2.0 copy-start.5
  203.8 1.0 copy-start.6
  238.6 2.0 copy-start.5
  240.6 1.0 copy-start.6
  243.3 4.0 copy-start.7
  243.3 4.8 %copy-start.8 = (f32[1152]{0:T(1024)S(1)}, f32[1152]{0:T(1024)}, u32[]{:S(2)}) copy-start(f32[1152]{0:T(1024)} %broadcast_add_fusion) | copy-start | bytes 13828
  243.3 4.8 %copy-start.9 = (f32[1152]{0:T(1024)S(1)}, f32[1152]{0:T(1024)}, u32[]{:S(2)}) copy-start(f32[1152]{0:T(1024)} %param.22) | copy-start | bytes 13828
  266.4 6.1 %copy-start.11 = (s32[8,8]{1,0:T(8,128)S(1)}, s32[8,8]{1,0:T(8,128)}, u32[]{:S(2)}) copy-start(s32[8,8]{1,0:T(8,128)} %param.18) | copy-start | bytes 772
  266.4 90.8 %all-to-all-start = ((bf16[2,256,3456]{2,0,1:T(2,128)(2,1)}), bf16[2,256,3456]{2,0,1:T(2,128)(2,1)S(1)}, u32[]{:S(2)}, u32[]{:S(2)}) async-start(bf16[2,256,3456]{2,0,1:T(2,128)(2,1)} %copy.54), calls=%async_computation | async-start | bytes 7077888 | tf_op jit(solution)/shard_map/all_to_all | solution.py:156
  379.2 1.6 copy-start.4
  383.5 42.7 %copy-start.1 = (bf16[2,8,32,1152]{3,2,1,0:T(8,128)(2,1)S(1)}, bf16[2,8,32,1152]{3,2,1,0:T(8,128)(2,1)}, u32[]{:S(2)}) copy-start(bf16[2,8,32,1152]{3,2,1,0:T(8,128)(2,1)} %param.13) | copy-start | bytes 3538948
Sparse Core Ops, SparseCore 0:
  10.1 117.6 all-gather.2
  130.6 122.0 all-gather.4
where the time goes:
time: 439 us; the launch traced here: 433 us
  waiting for transfers between devices  208 us (47%)
  local copies, waits for them, and re-layouts  101 us (23%)
  blocking collectives  38.1 us (9%)
  matrix products  35.6 us (8%)
  other arithmetic  27.8 us (6%)
  between operations  13.9 us (3%)
  starting transfers between devices  8.15 us (2%)
    ppermute x1, waiting for transfers between devices, padded(): lax.ppermute(lax.slice_in_dim(block, block.shape[dim] - width, None, axis...  108 us
    all_to_all x1, waiting for transfers between devices, local(): lax.all_to_all(projected, 'frame', split_axis=1, concat_axis=0, tiled=True)  84.6 us
    all_to_all x1, blocking collectives, local(): lax.all_to_all(temporal, 'frame', split_axis=0, concat_axis=1, tiled=True)  38.1 us
    dynamic_slice x8, local copies, waits for them, and re-layouts, local(): attended = lax.map(frame_window, (query_tiles, picked[0], picked[1]))  33.6 us
    dot_general x2, matrix products, fold_with(): return jnp.dot(left, piece, preferred_element_type=jnp.float32)  12.2 us
    dot_general x2, matrix products, window_attention(): jnp.einsum('thqk,tkhe->tqhe', weights, shaped_v, preferred_element_type=j...  10.6 us
    gather x1, local copies, waits for them, and re-layouts, local(): jnp.take(key_tiles, local_ids, axis=2)  9.72 us
    sub x2, other arithmetic, window_attention(): powers = jnp.exp(scores - peak)  9.18 us
  transfers between devices with their start and end apart: 5, of which 4 were waited for; matrix products, arithmetic and copies ran while one was open for 27% of the time, Pallas kernels for 0%

commit v1 on v0

--- a/solution.py
+++ b/solution.py
@@ -15,18 +15,27 @@
 EPS = 1e-06
 
 
-def padded(block, sides, width):
-    for axis, dim in sides:
-        count = lax.axis_size(axis)
-        forward = [(i, i + 1) for i in range(count - 1)]
-        forward.append((count - 1, 0))
-        backward = [(target, source) for source, target in forward]
-        low = lax.ppermute(
-            lax.slice_in_dim(block, block.shape[dim] - width, None, axis=dim), axis, forward
-        )
-        high = lax.ppermute(lax.slice_in_dim(block, 0, width, axis=dim), axis, backward)
-        block = jnp.concatenate([low, block, high], axis=dim)
-    return block
+ROW_AXIS = ("x", "zl")
+FRAME_AXIS = ("y", "zh", "core")
+
+
+def padded(block):
+    count = lax.axis_size(ROW_AXIS)
+    down = [(i, (i + 1) % count) for i in range(count) if (i + 1) % 4 != 3]
+    up = [(target, source) for source, target in down]
+    low = lax.ppermute(block, ROW_AXIS, down)
+    high = lax.ppermute(block, ROW_AXIS, up)
+    return jnp.concatenate([low, block, high], axis=2)
+
+
+def gathered(weight):
+    other = lax.ppermute(weight, ("zh", "zl"), [(i, 7 - i) for i in range(8)])
+    first = lax.axis_index("zh") == 0
+    pair = jnp.stack((jnp.where(first, weight, other), jnp.where(first, other, weight)), 0)
+    full = lax.all_gather(pair, ("y", "core"), axis=0, tiled=False)
+    rows, cols = weight.shape
+    full = full.reshape(4, 2, 2, rows, cols)
+    return jnp.transpose(full, (0, 2, 1, 3, 4)).reshape(16 * rows, cols)
 
 
 def tiles_of(field):
@@ -125,9 +134,9 @@
     tiles_wide = breadth // TILE
     tokens_here = frames_here * height * breadth
     stacked = jnp.stack((spatial_k, spatial_v), 0)
-    rims = padded(stacked, (("row", 2),), TILE)
+    rims = padded(stacked)
     key_tiles = tiles_of(rims)
-    tile_row_here = (lax.axis_index("row") + 1) % (ROWS // TILE)
+    tile_row_here = (lax.axis_index(ROW_AXIS) + 1) % (ROWS // TILE)
     local_ids = (
         (neighbour_list // tiles_wide - tile_row_here + 1) * tiles_wide
         + neighbour_list % tiles_wide
@@ -138,7 +147,7 @@
     query_tiles = tiles_of(spatial_q)
     attended = lax.map(frame_window, (query_tiles, picked[0], picked[1]))
     heads = untile(attended, height, breadth).reshape(tokens_here, channels)
-    spatial_sum = fold_with(heads, lax.all_gather(out_weight, "frame", axis=0, tiled=True))
+    spatial_sum = fold_with(heads, gathered(out_weight))
     mixed = (residual.reshape(tokens_here, channels).astype(jnp.float32) + spatial_sum).astype(
         jnp.bfloat16
     )
@@ -148,12 +157,11 @@
         + pos_embed[:, None, :]
     )
     normed = normalize(shifted, mod_shift, mod_scale).astype(jnp.bfloat16)
-    normed_rows = normed.reshape(tokens_here, channels)
-    projected = fold_with(
-        normed_rows, lax.all_gather(qkv_weight, "frame", axis=0, tiled=True)
-    ).astype(jnp.bfloat16)
-    projected = projected.reshape(frames_here, height * breadth, 3 * channels)
-    projected = lax.all_to_all(projected, "frame", split_axis=1, concat_axis=0, tiled=True)
+    normed = lax.all_to_all(normed, FRAME_AXIS, split_axis=1, concat_axis=0, tiled=True)
+    projected = fold_with(normed.reshape(tokens_here, channels), gathered(qkv_weight)).astype(
+        jnp.bfloat16
+    )
+    projected = projected.reshape(-1, tokens_here // 32, 3 * channels)
     allowed = jnp.repeat(jnp.repeat(block_mask, BLOCK, axis=0), BLOCK, axis=1) == 1
     temporal = frame_attention(
         projected[..., :channels],
@@ -161,27 +169,31 @@
         projected[..., 2 * channels :],
         allowed,
     )
-    returned = lax.all_to_all(temporal, "frame", split_axis=0, concat_axis=1, tiled=True)
+    returned = lax.all_to_all(temporal, FRAME_AXIS, split_axis=0, concat_axis=1, tiled=True)
     return returned.reshape(frames_here, height, breadth, channels)
 
 
 def solution(mesh):
+    fine = jax.sharding.Mesh(
+        mesh.devices.reshape(4, 2, 2, 4, 4), ("y", "zh", "core", "x", "zl")
+    )
+    tokens = P(FRAME_AXIS, ROW_AXIS, None, None)
     return jax.shard_map(
         local,
-        mesh=mesh,
+        mesh=fine,
         in_specs=(
-            P("frame", "row", None, None),
-            P("frame", "row", None, None),
-            P("frame", "row", None, None),
-            P("frame", "row", None, None),
-            P("row", None),
+            tokens,
+            tokens,
+            tokens,
+            tokens,
+            P(ROW_AXIS, None),
             P(),
-            P("frame", None),
-            P("frame", None),
-            P("frame", None),
+            P(FRAME_AXIS, None),
+            P(FRAME_AXIS, None),
+            P(FRAME_AXIS, None),
             P(),
             P(),
         ),
-        out_specs=P("frame", "row", None, None),
+        out_specs=tokens,
         check_vma=False,
     )

time: 439 us -> 386 us (0.88)
  waiting for transfers between devices: 208 us -> 143 us
  starting transfers between devices: 8.15 us -> 25.8 us
    all_to_all x1, waiting for transfers between devices: 84.6 us -> 33.8 us  [local(): lax.all_to_all(normed, FRAME_AXIS, split_axis=1, concat_axis=0, tiled=True)]
    ppermute x2 -> x4, starting transfers between devices: 2.03 us -> 17.9 us  [the longest x2 10.5 us: gathered(): other = lax.ppermute(weight, ('zh', 'zl'), [(i, 7 - i) for i in range(8)])]
    ppermute x2 -> x4, waiting for transfers between devices: 117 us -> 109 us  [the longest x2 109 us: gathered(): other = lax.ppermute(weight, ('zh', 'zl'), [(i, 7 - i) for i in range(8)])]
    transpose x0 -> x2, local copies, waits for them, and re-layouts: none -> 5.85 us  [gathered(): return jnp.transpose(full, (0, 2, 1, 3, 4)).reshape(16 * rows, cols)]
    reshape x1 -> x0, local copies, waits for them, and re-layouts: 5.39 us -> none  [local(): projected = projected.reshape(frames_here, height * breadth, 3 * channels)]
  transfers between devices with their start and end apart: 5 -> 7, of which waited for: 4 -> 3; matrix products, arithmetic and copies ran while one was open for 27% -> 32% of each run, Pallas kernels for 0% -> 0%
where the time goes in v1:
time: 386 us; the launch traced here: 384 us
  waiting for transfers between devices  143 us (37%)
  local copies, waits for them, and re-layouts  105 us (27%)
  blocking collectives  36 us (9%)
  matrix products  31.6 us (8%)
  other arithmetic  28.9 us (7%)
  starting transfers between devices  25.8 us (7%)
  between operations  13.7 us (4%)
    ppermute x2, waiting for transfers between devices, gathered(): other = lax.ppermute(weight, ('zh', 'zl'), [(i, 7 - i) for i in range(8)])  109 us
    all_to_all x1, blocking collectives, local(): lax.all_to_all(temporal, FRAME_AXIS, split_axis=0, concat_axis=1, tiled=T...  36 us
    all_to_all x1, waiting for transfers between devices, local(): lax.all_to_all(normed, FRAME_AXIS, split_axis=1, concat_axis=0, tiled=True)  33.8 us
    dynamic_slice x8, local copies, waits for them, and re-layouts, local(): attended = lax.map(frame_window, (query_tiles, picked[0], picked[1]))  33.7 us
    dot_general x2, matrix products, window_attention(): jnp.einsum('thqk,tkhe->tqhe', weights, shaped_v, preferred_element_type=j...  10.5 us
    ppermute x2, starting transfers between devices, gathered(): other = lax.ppermute(weight, ('zh', 'zl'), [(i, 7 - i) for i in range(8)])  10.5 us
    gather x1, local copies, waits for them, and re-layouts, local(): jnp.take(key_tiles, local_ids, axis=2)  10.4 us
    sub x2, other arithmetic, window_attention(): powers = jnp.exp(scores - peak)  9.13 us
  transfers between devices with their start and end apart: 7, of which 3 were waited for; matrix products, arithmetic and copies ran while one was open for 32% of the time, Pallas kernels for 0%

profile of v1, /device:TPU:38, one launch (start us, length us, event | category | flops | bytes accessed | tf_op | source)
XLA Modules:
  0.0 384.5 jit_solution(1866561831141859404)
XLA Ops:
  6.5 5.8 %collective-permute-start.2 = (bf16[72,1152]{1,0:T(8,128)(2,1)}, bf16[72,1152]{1,0:T(8,128)(2,1)S(1)}, u32[]{:S(2)}, u32[]{:S(2)}) collective-permute-start(bf16[72,1152]{1,0:T(8,128)(2,1)} %param.19), channel_id=1, source_target_pairs={{0,35},{1,34},{2,33},{3,32},{32,3},{33,2},{34,1},{35,0},{4,39},{5,... | collective-permute-start | bytes 497672 | tf_op jit(solution)/shard_map/ppermute | solution.py:32
  12.4 4.5 %collective-permute-done.2 = bf16[72,1152]{1,0:T(8,128)(2,1)S(1)} collective-permute-done((bf16[72,1152]{1,0:T(8,128)(2,1)}, bf16[72,1152]{1,0:T(8,128)(2,1)S(1)}, u32[]{:S(2)}, u32[]{:S(2)}) %collective-permute-start.2) | collective-permute-done | bytes 165920 | tf_op jit(solution)/shard_map/ppermute | solution.py:32
  24.6 4.5 %collective-permute-start.1 = (bf16[2,2,8,32,1152]{4,3,2,1,0:T(8,128)(2,1)}, bf16[2,2,8,32,1152]{4,3,2,1,0:T(8,128)(2,1)}, u32[]{:S(2)}, u32[]{:S(2)}) collective-permute-start(bf16[2,2,8,32,1152]{4,3,2,1,0:T(8,128)(2,1)} %pad_maximum_fusion.1), channel_id=1, source_target_pairs={{1,0},{2,1},{4,3},{5,4},{6,5},{8,7},{9,8},{10,9},{12,11},{13,12},{... | collective-permute-start | bytes 7077896 | tf_op jit(solution)/shard_map/ppermute | solution.py:27
  29.1 4.7 %collective-permute-start.3 = (bf16[72,3456]{1,0:T(8,128)(2,1)S(1)}, bf16[72,3456]{1,0:T(8,128)(2,1)S(1)}, u32[]{:S(2)}, u32[]{:S(2)}) collective-permute-start(bf16[72,3456]{1,0:T(8,128)(2,1)S(1)} %copy-done.7), channel_id=1, source_target_pairs={{0,35},{1,34},{2,33},{3,32},{32,3},{33,2},{34,1},{35,0},{4,39},{5,... | collective-permute-start | bytes 1493000 | tf_op jit(solution)/shard_map/ppermute | solution.py:32
  35.8 104.9 %collective-permute-done.3 = bf16[72,3456]{1,0:T(8,128)(2,1)S(1)} collective-permute-done((bf16[72,3456]{1,0:T(8,128)(2,1)S(1)}, bf16[72,3456]{1,0:T(8,128)(2,1)S(1)}, u32[]{:S(2)}, u32[]{:S(2)}) %collective-permute-start.3) | collective-permute-done | bytes 497696 | tf_op jit(solution)/shard_map/ppermute | solution.py:32
  145.4 4.0 %copy.95 = bf16[2,2,3,4,8,8,1152]{6,5,4,3,2,1,0:T(8,128)(2,1)} copy(bf16[2,2,3,4,8,8,1152]{6,5,3,4,2,1,0:T(8,128)(2,1)S(1)} %bitcast.93) | data formatting | bytes 14155776 | tf_op jit(solution)/shard_map/transpose | solution.py:53
  149.3 10.4 %gather_fusion = bf16[24,2,2,64,1152]{4,3,2,1,0:T(8,128)(2,1)} fusion(bf16[2,2,12,64,1152]{4,3,2,1,0:T(8,128)(2,1)} %bitcast.92, s32[1024]{0:T(1024)S(1)} %pad_clamp_fusion), kind=kCustom, calls=%fused_computation | custom fusion | bytes 28311648 | tf_op jit(solution)/shard_map/jit(_take)/gather | solution.py:144
  159.7 7.0 %select_bitcast_fusion = bf16[2,2,24,64,1152]{4,3,1,0,2:T(8,128)(2,1)S(1)} fusion(bf16[24,2,2,64,1152]{4,3,2,1,0:T(8,128)(2,1)} %gather_fusion, pred[24]{0:T(512)(128)(4,1)S(1)} %compare_and_fusion), kind=kLoop, calls=%fused_computation.18 | loop fusion | flops 7077888 | bytes 28311576 | tf_op jit(solution)/shard_map/jit(_take)/select_n | solution.py:144
  168.3 3.6 copy.96
  171.8 3.6 copy.98
  175.5 73.7 %while.10 = (s32[]{:T(128)}, bf16[2,4,64,1152]{3,2,1,0:T(8,128)(2,1)}, bf16[2,4,384,1152]{3,2,1,0:T(8,128)(2,1)}, bf16[2,4,64,1152]{3,2,1,0:T(8,128)(2,1)}, bf16[2,4,384,1152]{3,2,1,0:T(8,128)(2,1)}, /*index=5*/s32[]{:T(128)}) while((s32[]{:T(128)}, bf16[2,4,64,1152]{3,2,1,0:T(8,128)(2,1)}, bf16[2,4,384,1152]{3,2,1,0:T(8,128)(2,1)}, ...), condition=%wide.region_3.4_spmd, body=%wide.region_0.3_spmd.sunk | while | flops 462717312 | bytes 77103232 | solution.py:148
  175.5 5.6 %constant_dynamic-slice_fusion.5 = (bf16[1,4,384,1152]{3,2,1,0:T(8,128)(2,1)}, bf16[1,4,384,1152]{3,2,1,0:T(8,128)(2,1)S(1)}) fusion(bf16[2,4,384,1152]{3,2,1,0:T(8,128)(2,1)} %get-tuple-element.138, s32[]{:T(128)} %get-tuple-element.128, bf16[2,4,384,1152]{3,2,1,0:T(8,128)(2,1)} %get-tuple-element.136), kind=kLoop, calls=%fused_computation.13.clone.1 | loop fusion | bytes 14155780 | tf_op jit(solution)/shard_map/while/body/jit(dynamic_index_in_dim)/dynamic_slice | solution.py:148
  181.1 5.8 %copy.134 = bf16[1,4,384,1152]{2,3,1,0:T(8,128)(2,1)} copy(bf16[1,4,384,1152]{3,2,1,0:T(8,128)(2,1)} %get-tuple-element.119) | data formatting | bytes 7077888 | tf_op jit(solution)/shard_map/while/body/jit(dynamic_index_in_dim)/dynamic_slice | solution.py:148
  188.8 3.7 reshape.191
  195.9 4.6 %fusion.56 = (f32[4,16,64]{2,1,0:T(8,128)}, f32[4,16,64,384]{3,2,1,0:T(8,128)}) fusion(f32[4,16,64,384]{3,2,1,0:T(8,128)S(1)} %fusion.55), kind=kOutput, calls=%fused_computation.72.clone.1 | output fusion | flops 6291839 | bytes 12599296 | tf_op jit(solution)/shard_map/while/body/eval_jaxpr/sub | solution.py:82
  200.5 3.6 copy.133
  204.1 5.3 %fusion.57 = bf16[4,64,16,72]{3,1,2,0:T(8,128)(2,1)S(1)} fusion(bf16[4,384,16,72]{1,3,2,0:T(8,128)(2,1)} %bitcast.89, f32[4,16,64,384]{3,2,1,0:T(8,128)} %get-tuple-element.120, f32[4,16,64]{2,1,0:T(8,128)} %get-tuple-element.121), kind=kOutput, calls=%fused_computation.9.clone.1 | convolution fusion | flops 229933056 | bytes 10436608 | tf_op jit(solution)/shard_map/while/body/eval_jaxpr/thqk,tkhe->tqhe/dot_general | solution.py:84
  212.4 5.5 %constant_dynamic-slice_fusion.5 = (bf16[1,4,384,1152]{3,2,1,0:T(8,128)(2,1)}, bf16[1,4,384,1152]{3,2,1,0:T(8,128)(2,1)S(1)}) fusion(bf16[2,4,384,1152]{3,2,1,0:T(8,128)(2,1)} %get-tuple-element.138, s32[]{:T(128)} %get-tuple-element.128, bf16[2,4,384,1152]{3,2,1,0:T(8,128)(2,1)} %get-tuple-element.136), kind=kLoop, calls=%fused_computation.13.clone.1 | loop fusion | bytes 14155780 | tf_op jit(solution)/shard_map/while/body/jit(dynamic_index_in_dim)/dynamic_slice | solution.py:148
  217.9 5.8 %copy.134 = bf16[1,4,384,1152]{2,3,1,0:T(8,128)(2,1)} copy(bf16[1,4,384,1152]{3,2,1,0:T(8,128)(2,1)} %get-tuple-element.119) | data formatting | bytes 7077888 | tf_op jit(solution)/shard_map/while/body/jit(dynamic_index_in_dim)/dynamic_slice | solution.py:148
  225.6 3.7 reshape.191
  232.6 4.6 %fusion.56 = (f32[4,16,64]{2,1,0:T(8,128)}, f32[4,16,64,384]{3,2,1,0:T(8,128)}) fusion(f32[4,16,64,384]{3,2,1,0:T(8,128)S(1)} %fusion.55), kind=kOutput, calls=%fused_computation.72.clone.1 | output fusion | flops 6291839 | bytes 12599296 | tf_op jit(solution)/shard_map/while/body/eval_jaxpr/sub | solution.py:82
  237.2 3.6 copy.133
  240.8 5.3 %fusion.57 = bf16[4,64,16,72]{3,1,2,0:T(8,128)(2,1)S(1)} fusion(bf16[4,384,16,72]{1,3,2,0:T(8,128)(2,1)} %bitcast.89, f32[4,16,64,384]{3,2,1,0:T(8,128)} %get-tuple-element.120, f32[4,16,64]{2,1,0:T(8,128)} %get-tuple-element.121), kind=kOutput, calls=%fused_computation.9.clone.1 | convolution fusion | flops 229933056 | bytes 10436608 | tf_op jit(solution)/shard_map/while/body/eval_jaxpr/thqk,tkhe->tqhe/dot_general | solution.py:84
  258.2 7.9 %all-to-all-start = ((bf16[2,256,1152]{2,0,1:T(2,128)(2,1)}), bf16[2,256,1152]{2,0,1:T(2,128)(2,1)S(1)}, u32[]{:S(2)}, u32[]{:S(2)}) async-start(bf16[2,256,1152]{2,0,1:T(2,128)(2,1)} %copy.103), calls=%async_computation | async-start | bytes 2359296 | tf_op jit(solution)/shard_map/all_to_all | solution.py:160
  266.1 33.8 %all-to-all-done = bf16[2,256,1152]{2,0,1:T(2,128)(2,1)S(1)} async-done(((bf16[2,256,1152]{2,0,1:T(2,128)(2,1)}), bf16[2,256,1152]{2,0,1:T(2,128)(2,1)S(1)}, u32[]{:S(2)}, u32[]{:S(2)}) %all-to-all-start) | async-done | bytes 1179680 | tf_op jit(solution)/shard_map/all_to_all | solution.py:160
  301.2 3.8 copy.106
  305.0 6.5 %convolution_convert_fusion = bf16[512,3456]{1,0:T(8,128)(2,1)S(1)} fusion(bf16[512,1152]{1,0:T(8,128)(2,1)} %bitcast.108, bf16[1152,3456]{1,0:T(8,128)(2,1)S(1)} %bitcast.96), kind=kOutput, calls=%fused_computation.20 | convolution fusion | flops 4078632960 | bytes 12681216 | tf_op jit(solution)/shard_map/dot_general | solution.py:113
  313.1 5.0 %reshape.173 = bf16[32,16,16,72]{3,2,1,0:T(8,128)(2,1)S(1)} reshape(bf16[32,16,1152]{2,1,0:T(8,128)(2,1)} %get-tuple-element.76) | data formatting | bytes 2359296 | tf_op jit(solution)/shard_map/reshape | solution.py:91
  318.1 5.7 %reshape.174 = bf16[32,16,16,72]{3,2,1,0:T(8,128)(2,1)} reshape(bf16[32,16,1152]{2,1,0:T(8,128)(2,1)} %get-tuple-element.75) | data formatting | bytes 2359296 | tf_op jit(solution)/shard_map/reshape | solution.py:92
  323.9 4.7 %reshape.172 = bf16[32,16,16,72]{3,2,1,0:T(8,128)(2,1)} reshape(bf16[32,16,1152]{2,1,0:T(8,128)(2,1)S(1)} %get-tuple-element.74) | data formatting | bytes 2359296 | tf_op jit(solution)/shard_map/reshape | solution.py:93
  328.5 4.3 %fusion.17 = f32[16,16,32,32]{2,3,1,0:T(8,128)S(1)} fusion(bf16[32,16,16,72]{3,2,1,0:T(8,128)(2,1)} %reshape.174, bf16[32,16,16,72]{3,2,1,0:T(8,128)(2,1)S(1)} %reshape.173), kind=kOutput, calls=%fused_computation.34 | convolution fusion | flops 37748736 | bytes 3407872 | tf_op jit(solution)/shard_map/fphe,gphe->phfg/dot_general | solution.py:94
  340.5 36.0 %all_to_all.30 = bf16[32,16,1152]{2,1,0:T(8,128)(2,1)S(1)} all-to-all(bf16[32,16,1152]{2,1,0:T(8,128)(2,1)} %reshape.175), channel_id=1, replica_groups=mesh['y'=4,'zh'=2,'core'=2,'x'=4,'zl'=4] {'y','zh','core'}, dimensions={0} | all-to-all | bytes 2359296 | tf_op jit(solution)/shard_map/all_to_all | solution.py:172
  (92 shorter events, 53.2 us)
Async XLA Ops:
  6.5 28.1 %copy-start = (bf16[2,8,32,1152]{3,2,1,0:T(8,128)(2,1)S(1)}, bf16[2,8,32,1152]{3,2,1,0:T(8,128)(2,1)}, u32[]{:S(2)}) copy-start(bf16[2,8,32,1152]{3,2,1,0:T(8,128)(2,1)} %param.13) | copy-start | bytes 3538948
  6.5 12.2 %copy-start.2 = (bf16[2,8,32,1152]{3,2,1,0:T(8,128)(2,1)S(1)}, bf16[2,8,32,1152]{3,2,1,0:T(8,128)(2,1)}, u32[]{:S(2)}) copy-start(bf16[2,8,32,1152]{3,2,1,0:T(8,128)(2,1)} %param.15) | copy-start | bytes 3538948
  6.5 244.0 %all-gather.5.cloned.1.call-start = ((), (), s32[]{:S(2)}) async-start(), calls=%async_computation.2 | async-start | bytes 2985984 | tf_op jit(solution)/shard_map/all_gather | solution.py:35
  6.5 10.4 %collective-permute-start.2 = (bf16[72,1152]{1,0:T(8,128)(2,1)}, bf16[72,1152]{1,0:T(8,128)(2,1)S(1)}, u32[]{:S(2)}, u32[]{:S(2)}) collective-permute-start(bf16[72,1152]{1,0:T(8,128)(2,1)} %param.19), channel_id=1, source_target_pairs={{0,35},{1,34},{2,33},{3,32},{32,3},{33,2},{34,1},{35,0},{4,39},{5,... | collective-permute-start | bytes 497672 | tf_op jit(solution)/shard_map/ppermute | solution.py:32
  18.7 282.5 %all-gather.7.cloned.1.call-start = ((), (), s32[]{:S(2)}) async-start(), calls=%async_computation.3 | async-start | bytes 8957952 | tf_op jit(solution)/shard_map/all_gather | solution.py:35
  18.8 10.4 %copy-start.7 = (bf16[72,3456]{1,0:T(8,128)(2,1)S(1)}, bf16[72,3456]{1,0:T(8,128)(2,1)}, u32[]{:S(2)}) copy-start(bf16[72,3456]{1,0:T(8,128)(2,1)} %param.20) | copy-start | bytes 1492996
  18.8 15.0 %copy-start.13 = (s32[4,6]{1,0:T(4,128)S(1)}, s32[4,6]{1,0:T(4,128)}, u32[]{:S(2)}) copy-start(s32[4,6]{1,0:T(4,128)} %param.17) | copy-start | bytes 292
  18.8 15.3 %copy-start.11 = (f32[1152]{0:T(1024)S(1)}, f32[1152]{0:T(1024)}, u32[]{:S(2)}) copy-start(f32[1152]{0:T(1024)} %param.23) | copy-start | bytes 13828
  21.7 120.1 %collective-permute-start = (bf16[2,2,8,32,1152]{4,3,2,1,0:T(8,128)(2,1)}, bf16[2,2,8,32,1152]{4,3,2,1,0:T(8,128)(2,1)}, u32[]{:S(2)}, u32[]{:S(2)}) collective-permute-start(bf16[2,2,8,32,1152]{4,3,2,1,0:T(8,128)(2,1)} %pad_maximum_fusion.1), channel_id=1, source_target_pairs={{0,1},{1,2},{3,4},{4,5},{5,6},{7,8},{8,9},{9,10},{11,12},{12,13},{... | collective-permute-start | bytes 7077896 | tf_op jit(solution)/shard_map/ppermute | solution.py:26
  24.6 117.2 %collective-permute-start.1 = (bf16[2,2,8,32,1152]{4,3,2,1,0:T(8,128)(2,1)}, bf16[2,2,8,32,1152]{4,3,2,1,0:T(8,128)(2,1)}, u32[]{:S(2)}, u32[]{:S(2)}) collective-permute-start(bf16[2,2,8,32,1152]{4,3,2,1,0:T(8,128)(2,1)} %pad_maximum_fusion.1), channel_id=1, source_target_pairs={{1,0},{2,1},{4,3},{5,4},{6,5},{8,7},{9,8},{10,9},{12,11},{13,12},{... | collective-permute-start | bytes 7077896 | tf_op jit(solution)/shard_map/ppermute | solution.py:27
  29.1 111.5 %collective-permute-start.3 = (bf16[72,3456]{1,0:T(8,128)(2,1)S(1)}, bf16[72,3456]{1,0:T(8,128)(2,1)S(1)}, u32[]{:S(2)}, u32[]{:S(2)}) collective-permute-start(bf16[72,3456]{1,0:T(8,128)(2,1)S(1)} %copy-done.7), channel_id=1, source_target_pairs={{0,35},{1,34},{2,33},{3,32},{32,3},{33,2},{34,1},{35,0},{4,39},{5,... | collective-permute-start | bytes 1493000 | tf_op jit(solution)/shard_map/ppermute | solution.py:32
  35.8 106.1 %copy-start.3 = (bf16[2,8,32,1152]{3,2,1,0:T(8,128)(2,1)S(1)}, bf16[2,8,32,1152]{3,2,1,0:T(8,128)(2,1)}, u32[]{:S(2)}) copy-start(bf16[2,8,32,1152]{3,2,1,0:T(8,128)(2,1)} %param.14) | copy-start | bytes 3538948
  209.3 2.0 copy-start.5
  211.4 1.0 copy-start.6
  246.0 2.0 copy-start.5
  248.1 1.0 copy-start.6
  250.5 2.1 copy-start.14
  252.6 1.9 copy-start.8
  254.5 0.9 copy-start.9
  254.5 0.9 copy-start.10
  255.9 10.1 %copy-start.12 = (s32[8,8]{1,0:T(8,128)S(1)}, s32[8,8]{1,0:T(8,128)}, u32[]{:S(2)}) copy-start(s32[8,8]{1,0:T(8,128)} %param.18) | copy-start | bytes 772
  258.2 41.8 %all-to-all-start = ((bf16[2,256,1152]{2,0,1:T(2,128)(2,1)}), bf16[2,256,1152]{2,0,1:T(2,128)(2,1)S(1)}, u32[]{:S(2)}, u32[]{:S(2)}) async-start(bf16[2,256,1152]{2,0,1:T(2,128)(2,1)} %copy.103), calls=%async_computation | async-start | bytes 2359296 | tf_op jit(solution)/shard_map/all_to_all | solution.py:160
  332.9 1.6 copy-start.4
  337.1 40.5 %copy-start.1 = (bf16[2,8,32,1152]{3,2,1,0:T(8,128)(2,1)S(1)}, bf16[2,8,32,1152]{3,2,1,0:T(8,128)(2,1)}, u32[]{:S(2)}) copy-start(bf16[2,8,32,1152]{3,2,1,0:T(8,128)(2,1)} %param.13) | copy-start | bytes 3538948
Sparse Core Ops, SparseCore 0:
  18.8 31.6 all-gather.4
  142.0 51.9 all-gather.6
